TPU v7x, 32 devices: a whole 2x2x4 slice. The times are simulated.
32 devices in a mesh: dp: 4 (over y, x), expert: 8 (over z, core).
Axes of the slice: x: 2, y: 2, z: 4, core: 2. Of those that a mesh axis runs over, the one named last changes fastest.
Arguments:
- tokens: bfloat16 [256, 3584], P('expert', 'dp'), may hold values from -6 to 6
- upstream: bfloat16 [256, 3584], P('expert', 'dp'), may hold values from -6 to 6
- expert_ids: int32 [256, 8], P('expert'), may hold values from 0 to 31, all different within a row
- gates: float32 [256, 8], P('expert'), may hold values from 0.2 to 1
- hot: int32 [8], replicated, may hold values from 0 to 1, as said below
- w_in: bfloat16 [8, 3584, 2048], P('expert', 'dp'), may hold values from -0.09375 to 0.09375
- w_down: bfloat16 [8, 1024, 3584], P('expert', None, 'dp'), may hold values from -0.1875 to 0.1875
Outputs:
- layer_out: bfloat16 [256, 3584], P('expert', 'dp')
- token_grad: bfloat16 [256, 3584], P('expert', 'dp')
- grad_in: bfloat16 [8, 3584, 2048], P('expert', 'dp')
- grad_down: bfloat16 [8, 1024, 3584], P('expert', None, 'dp')
Inputs may be any that keep to these rules, and one draw needn't show every extreme that they name: `expert_ids`: each row names 8 different experts; only those below 8 are computed by this layer. Every expert below 4 is hot; the others may or may not be.
All inputs are finite; a program needn't handle non-finite values.
Results may differ from a plain program's by a relative error of at most 0.028.
Values may be sent and summed in bfloat16 or wider, within the bound.
No kernel may reach another device: no remote copies, remote signals or barrier semaphores. Data moves between devices by JAX's collectives and lax.ppermute only.
A program may use at most 64 MiB of HBM per device.

v0:
```python
import jax
import jax.numpy as jnp
from jax import lax
from jax.sharding import PartitionSpec as P

CAP = 2


def plan_block(flat_ids, hot, expert_count, capacity):
    expert_lane = jnp.arange(expert_count, dtype=jnp.int32)
    in_window = flat_ids < expert_count
    chosen = ((flat_ids[:, None] == expert_lane[None, :]) & in_window[:, None]).astype(jnp.int32)
    occurrence = jnp.sum((jnp.cumsum(chosen, axis=0) - chosen) * chosen, axis=1)
    marked = jnp.sum(chosen * hot[None, :], axis=1)
    replica = (marked > 0) & (occurrence % 2 == 1)
    expert = jnp.where(in_window, flat_ids, 0)
    host_column = jnp.where(replica, (expert + expert_count // 2) % expert_count, expert)
    region_key = host_column + replica.astype(jnp.int32) * expert_count
    key_lane = jnp.arange(2 * expert_count, dtype=jnp.int32)
    keyed = ((region_key[:, None] == key_lane[None, :]) & in_window[:, None]).astype(jnp.int32)
    slot_rank = jnp.sum((jnp.cumsum(keyed, axis=0) - keyed) * keyed, axis=1)
    retained = in_window & (slot_rank < capacity)
    return (expert, host_column, slot_rank, replica, retained)


def fill_slots(position, total_slots):
    counts = position.shape[0]
    slot_index = jnp.full((total_slots + 1,), counts, jnp.int32)
    slot_index = slot_index.at[position].set(jnp.arange(counts, dtype=jnp.int32))
    return slot_index[:total_slots]


def pack_rows(slot_index, tokens, upstream, flat_gates, top_count):
    counts = flat_gates.shape[0]
    usable = slot_index < counts
    safe_index = jnp.where(usable, slot_index, 0)
    token_row = safe_index // top_count
    rows_in = jnp.where(usable[:, None], tokens[token_row], jnp.zeros((), jnp.bfloat16))
    scaled = flat_gates[safe_index][:, None] * upstream[token_row].astype(jnp.float32)
    rows_grad = jnp.where(usable[:, None], scaled, 0.0).astype(jnp.bfloat16)
    return (rows_in, rows_grad)


def activate(projected):
    half_width = projected.shape[1] // 2
    gate_part = projected[:, :half_width]
    up_part = projected[:, half_width:]
    sigmoid_gate = jax.nn.sigmoid(gate_part)
    hidden = (gate_part * sigmoid_gate * up_part).astype(jnp.bfloat16)
    return (gate_part, up_part, sigmoid_gate, hidden)


def pair_grads(hidden_grad, gate_part, up_part, sigmoid_gate):
    gate_grad = hidden_grad * up_part * sigmoid_gate * (1.0 + gate_part * (1.0 - sigmoid_gate))
    up_grad = hidden_grad * gate_part * sigmoid_gate
    return jnp.concatenate([gate_grad, up_grad], axis=1).astype(jnp.bfloat16)


def contract_last(left, right):
    return lax.dot_general(
        left, right, (((1,), (1,)), ((), ())), preferred_element_type=jnp.float32
    )


def contract_first(left, right):
    return lax.dot_general(
        left, right, (((0,), (0,)), ((), ())), preferred_element_type=jnp.float32
    )


def body(tokens, upstream, expert_ids, gates, hot, w_in, w_down):
    expert_count = hot.shape[0]
    token_count, top_count = expert_ids.shape
    share = tokens.shape[1]
    region_slots = expert_count * CAP
    total_slots = 2 * region_slots
    flat_gates = gates.reshape(-1)
    expert, host_column, slot_rank, replica, retained = plan_block(
        expert_ids.reshape(-1), hot, expert_count, CAP
    )
    own_in = w_in[0]
    own_down = w_down[0]
    far_in, far_down = (own_in, own_down)
    position = jnp.where(
        retained, expert * (2 * CAP) + replica.astype(jnp.int32) * CAP + slot_rank, total_slots
    )
    rows_in, rows_grad = pack_rows(
        fill_slots(position, total_slots), tokens, upstream, flat_gates, top_count
    )
    sent = (
        lax.all_to_all(
            rows_in.reshape(expert_count, 2, CAP, share),
            "expert",
            split_axis=0,
            concat_axis=0,
            tiled=True,
        ),
        lax.all_to_all(
            rows_grad.reshape(expert_count, 2, CAP, share),
            "expert",
            split_axis=0,
            concat_axis=0,
            tiled=True,
        ),
    )
    near_rows = sent[0][:, 0].reshape(region_slots, share)
    far_rows = sent[0][:, 1].reshape(region_slots, share)
    near_grad = sent[1][:, 0].reshape(region_slots, share)
    far_grad = sent[1][:, 1].reshape(region_slots, share)
    proj_part = jnp.concatenate(
        [
            jnp.dot(near_rows, own_in, preferred_element_type=jnp.float32),
            jnp.dot(far_rows, far_in, preferred_element_type=jnp.float32),
        ],
        axis=0,
    )
    grad_part = jnp.concatenate(
        [contract_last(near_grad, own_down), contract_last(far_grad, far_down)], axis=0
    )
    projected, hidden_grad = (
        lax.psum(proj_part.astype(jnp.bfloat16), "dp").astype(jnp.float32),
        lax.psum(grad_part.astype(jnp.bfloat16), "dp").astype(jnp.float32),
    )
    gate_part, up_part, sigmoid_gate, hidden = activate(projected)
    pair_grad = pair_grads(hidden_grad, gate_part, up_part, sigmoid_gate)
    near_hidden = hidden[:region_slots]
    far_hidden = hidden[region_slots:]
    near_pair = pair_grad[:region_slots]
    far_pair = pair_grad[region_slots:]
    out_near = jnp.dot(near_hidden, own_down, preferred_element_type=jnp.float32).astype(
        jnp.bfloat16
    )
    out_far = jnp.dot(far_hidden, far_down, preferred_element_type=jnp.float32).astype(jnp.bfloat16)
    input_near = contract_last(near_pair, own_in).astype(jnp.bfloat16)
    input_far = contract_last(far_pair, far_in).astype(jnp.bfloat16)
    near_in_grad = contract_first(near_rows, near_pair)
    near_down_grad = contract_first(near_hidden, near_grad)
    far_in_grad = contract_first(far_rows, far_pair).astype(jnp.bfloat16)
    far_down_grad = contract_first(far_hidden, far_grad).astype(jnp.bfloat16)
    back_in, back_down = lax.optimization_barrier((far_in_grad, far_down_grad))
    grad_in = (near_in_grad + back_in.astype(jnp.float32)).astype(jnp.bfloat16)
    grad_down = (near_down_grad + back_down.astype(jnp.float32)).astype(jnp.bfloat16)
    out_rows = jnp.stack(
        [out_near.reshape(expert_count, CAP, share), out_far.reshape(expert_count, CAP, share)],
        axis=1,
    )
    input_rows = jnp.stack(
        [input_near.reshape(expert_count, CAP, share), input_far.reshape(expert_count, CAP, share)],
        axis=1,
    )
    back = (
        lax.all_to_all(out_rows, "expert", split_axis=0, concat_axis=0, tiled=True),
        lax.all_to_all(input_rows, "expert", split_axis=0, concat_axis=0, tiled=True),
    )
    returned_out = back[0].reshape(total_slots, share)
    returned_input = back[1].reshape(total_slots, share)
    safe_lookup = jnp.where(retained, position, 0)
    picked_out = jnp.where(retained[:, None], returned_out[safe_lookup].astype(jnp.float32), 0.0)
    picked_input = jnp.where(
        retained[:, None], returned_input[safe_lookup].astype(jnp.float32), 0.0
    )
    weighted = (picked_out * flat_gates[:, None]).reshape(token_count, top_count, share)
    layer_out = jnp.sum(weighted, axis=1).astype(jnp.bfloat16)
    token_grad = jnp.sum(picked_input.reshape(token_count, top_count, share), axis=1).astype(
        jnp.bfloat16
    )
    return (layer_out, token_grad, grad_in[None], grad_down[None])


def solution(mesh):
    return jax.shard_map(
        body,
        mesh=mesh,
        in_specs=(
            P("expert", "dp"),
            P("expert", "dp"),
            P("expert", None),
            P("expert", None),
            P(),
            P("expert", "dp", None),
            P("expert", None, "dp"),
        ),
        out_specs=(
            P("expert", "dp"),
            P("expert", "dp"),
            P("expert", "dp", None),
            P("expert", None, "dp"),
        ),
        check_vma=False,
    )
```

profile of v0, /device:TPU:0, one launch (start us, length us, event | category | flops | bytes accessed | tf_op | source)
XLA Modules:
  0.0 121.8 jit_solution(12306745262388308910)
XLA Ops:
  7.2 0.9 copy.24
  8.4 0.6 reduce-window.14
  9.0 0.2 slice_reduce_fusion.1
  9.2 0.8 select_reduce_fusion
  10.0 0.6 reduce-window.16
  10.6 0.2 slice_reduce_fusion
  10.8 0.1 fusion.57
  11.0 1.4 %scatter_custom_fusion = s32[33]{0:T(128)S(1)} fusion(s32[256]{0:T(256)S(1)} %bitcast.102, s32[256]{0:T(256)S(1)} %iota.19, s32[]{:T(128)} %constant.64.clone.1), kind=kCustom, calls=%fused_computation.135 | custom fusion | bytes 136 | tf_op jit(solution)/shard_map/scatter | solution.py:29
  12.4 1.5 %gather_fusion = bf16[32,896]{1,0:T(8,128)(2,1)S(1)} fusion(bf16[32,896]{1,0:T(8,128)(2,1)} %param.7, s32[1024]{0:T(1024)S(1)} %get-tuple-element.28), kind=kCustom, calls=%fused_computation | custom fusion | bytes 114816 | tf_op jit(solution)/shard_map/gather | solution.py:38
  14.0 0.1 lt.116
  14.1 0.8 broadcast_select_fusion
  14.8 6.4 %all-to-all-start = ((bf16[8,2,2,896]{3,2,1,0:T(2,128)(2,1)}), bf16[8,2,2,896]{3,2,1,0:T(2,128)(2,1)S(1)}, u32[]{:S(2)}, u32[]{:S(2)}) async-start(bf16[8,2,2,896]{3,2,1,0:T(2,128)(2,1)} %broadcast_select_fusion), calls=%async_computation | async-start | bytes 114688 | tf_op jit(solution)/shard_map/all_to_all | solution.py:91
  21.2 1.5 %gather_fusion.3 = bf16[32,896]{1,0:T(8,128)(2,1)S(1)} fusion(bf16[32,896]{1,0:T(8,128)(2,1)} %param.8, s32[1024]{0:T(1024)S(1)} %get-tuple-element.28), kind=kCustom, calls=%fused_computation.3 | custom fusion | bytes 114816 | tf_op jit(solution)/shard_map/gather | solution.py:39
  22.8 0.8 copy.31
  23.6 0.7 gather_fusion.2
  24.3 0.1 mul.92
  24.5 0.8 select_convert_fusion
  25.3 1.8 %all-to-all-done = bf16[8,2,2,896]{3,2,1,0:T(2,128)(2,1)S(1)} async-done(((bf16[8,2,2,896]{3,2,1,0:T(2,128)(2,1)}), bf16[8,2,2,896]{3,2,1,0:T(2,128)(2,1)S(1)}, u32[]{:S(2)}, u32[]{:S(2)}) %all-to-all-start) | async-done | bytes 57376 | tf_op jit(solution)/shard_map/all_to_all | solution.py:91
  27.1 3.3 %all-to-all-start.2 = ((bf16[8,2,2,896]{3,2,1,0:T(2,128)(2,1)}), bf16[8,2,2,896]{3,2,1,0:T(2,128)(2,1)S(1)}, u32[]{:S(2)}, u32[]{:S(2)}) async-start(bf16[8,2,2,896]{3,2,1,0:T(2,128)(2,1)} %select_convert_fusion), calls=%async_computation.2 | async-start | bytes 114688 | tf_op jit(solution)/shard_map/all_to_all | solution.py:98
  30.6 2.8 %fusion.12 = bf16[16,2048]{1,0:T(8,128)(2,1)S(1)} fusion(bf16[16,896]{1,0:T(8,128)(2,1)S(1)} %reshape_squeeze.13, bf16[1,896,2048]{2,1,0:T(8,128)(2,1)} %param.12), kind=kOutput, calls=%fused_computation.19 | convolution fusion | flops 58753024 | bytes 3764224 | tf_op jit(solution)/shard_map/dot_general | solution.py:113
  33.4 0.4 copy-done.1
  33.7 0.6 fusion.9
  34.3 2.0 %all-to-all-done.2 = bf16[8,2,2,896]{3,2,1,0:T(2,128)(2,1)S(1)} async-done(((bf16[8,2,2,896]{3,2,1,0:T(2,128)(2,1)}), bf16[8,2,2,896]{3,2,1,0:T(2,128)(2,1)S(1)}, u32[]{:S(2)}, u32[]{:S(2)}) %all-to-all-start.2) | async-done | bytes 57376 | tf_op jit(solution)/shard_map/all_to_all | solution.py:98
  36.4 0.6 fusion.24
  36.9 0.6 fusion.27
  37.5 0.7 pad_maximum_fusion
  38.2 0.6 pad_maximum_fusion.2
  38.9 42.2 %all-reduce.3.cloned.1.call-done = (bf16[32,1024]{1,0:T(8,128)(2,1)}, bf16[32,2048]{1,0:T(8,128)(2,1)}) async-done(((bf16[32,1024]{1,0:T(8,128)(2,1)}, bf16[32,2048]{1,0:T(8,128)(2,1)}), (bf16[32,1024]{1,0:T(8,128)(2,1)}, bf16[32,2048]{1,0:T(8,128)(2,1)})) %all-reduce.3.cloned.1.call-update) | async-done | bytes 196624 | tf_op jit(solution)/shard_map/psum | solution.py:122
  81.1 0.9 convert_element_type.93
  82.0 0.9 fusion.47
  82.9 1.9 %convolution_convert_fusion.1 = bf16[1024,896]{1,0:T(8,128)(2,1)} fusion(bf16[16,896]{1,0:T(8,128)(2,1)S(1)} %reshape_squeeze.15, bf16[32,1024]{1,0:T(8,128)(2,1)S(1)} %get-tuple-element.20), kind=kOutput, calls=%fused_computation.28 | convolution fusion | flops 30277632 | bytes 1896448 | tf_op jit(solution)/shard_map/dot_general | solution.py:66
  84.8 0.3 fusion.30
  85.2 0.4 fusion.33
  85.5 1.2 convolution_convert_fusion
  86.7 0.2 copy-done.2
  86.9 1.0 fusion.36
  87.9 1.1 fusion.39
  89.0 3.0 %fusion.8 = bf16[1,896,2048]{2,1,0:T(8,128)(2,1)} fusion(bf16[896,2048]{1,0:T(8,128)(2,1)S(1)} %convolution_convert_fusion, bf16[16,896]{1,0:T(8,128)(2,1)S(1)} %reshape_squeeze.12, bf16[32,1024]{1,0:T(8,128)(2,1)S(1)} %get-tuple-element.18, bf16[32,1024]{1,0:T(8,128)(2,1)S(1)} %get-tuple-element.19), kind=kOutput, calls=%fused_computation.17 | convolution fusion | flops 64356352 | bytes 7499776 | tf_op jit(solution)/shard_map/dot_general | solution.py:66
  92.0 0.7 pad_maximum_fusion.3
  92.7 4.6 %all-to-all-start.1 = ((bf16[8,2,2,896]{3,2,1,0:T(2,128)(2,1)}), bf16[8,2,2,896]{3,2,1,0:T(2,128)(2,1)S(1)}, u32[]{:S(2)}, u32[]{:S(2)}) async-start(bf16[8,2,2,896]{3,2,1,0:T(2,128)(2,1)} %pad_maximum_fusion.3), calls=%async_computation.1 | async-start | bytes 114688 | tf_op jit(solution)/shard_map/all_to_all | solution.py:152
  97.4 0.7 pad_maximum_fusion.4
  98.1 5.1 %all-to-all-done.1 = bf16[8,2,2,896]{3,2,1,0:T(2,128)(2,1)S(1)} async-done(((bf16[8,2,2,896]{3,2,1,0:T(2,128)(2,1)}), bf16[8,2,2,896]{3,2,1,0:T(2,128)(2,1)S(1)}, u32[]{:S(2)}, u32[]{:S(2)}) %all-to-all-start.1) | async-done | bytes 57376 | tf_op jit(solution)/shard_map/all_to_all | solution.py:152
  103.2 3.5 %all-to-all-start.3 = ((bf16[8,2,2,896]{3,2,1,0:T(2,128)(2,1)}), bf16[8,2,2,896]{3,2,1,0:T(2,128)(2,1)S(1)}, u32[]{:S(2)}, u32[]{:S(2)}) async-start(bf16[8,2,2,896]{3,2,1,0:T(2,128)(2,1)} %pad_maximum_fusion.4), calls=%async_computation.3 | async-start | bytes 114688 | tf_op jit(solution)/shard_map/all_to_all | solution.py:153
  106.8 3.4 %fusion.23 = bf16[1,1024,896]{2,1,0:T(8,128)(2,1)} fusion(bf16[1024,896]{1,0:T(8,128)(2,1)} %convolution_convert_fusion.1, bf16[16,896]{1,0:T(8,128)(2,1)S(1)} %reshape_squeeze.14, bf16[32,1024]{1,0:T(8,128)(2,1)S(1)} %get-tuple-element.20), kind=kOutput, calls=%fused_computation.29 | convolution fusion | flops 32112640 | bytes 3731456 | tf_op jit(solution)/shard_map/dot_general | solution.py:66
  110.2 1.2 gather_fusion.1
  111.4 1.0 all-to-all-done.3
  112.4 1.2 gather_fusion.4
  113.6 1.3 %fusion.42 = (bf16[32,896]{1,0:T(8,128)(2,1)}, bf16[32,896]{1,0:T(8,128)(2,1)}) fusion(bf16[256,896]{1,0:T(8,128)(2,1)S(1)} %gather_fusion.4, pred[32,8]{1,0:T(8,128)(4,1)S(1)} %compare_and_fusion, f32[32,8]{1,0:T(8,128)S(1)} %copy.31, bf16[256,896]{1,0:T(8,128)(2,1)S(1)} %gather_fusion.1), kind=kLoop, calls=%fused_computation.37 | loop fusion | flops 1548288 | bytes 1033472 | tf_op jit(solution)/shard_map/reduce_sum | solution.py:164
  (44 shorter events, 1.1 us)
Async XLA Ops:
  7.2 29.2 %copy-start = (bf16[1,1024,896]{2,1,0:T(8,128)(2,1)S(1)}, bf16[1,1024,896]{2,1,0:T(8,128)(2,1)}, u32[]{:S(2)}) copy-start(bf16[1,1024,896]{2,1,0:T(8,128)(2,1)} %param.13) | copy-start | bytes 5505028
  14.8 12.2 %all-to-all-start = ((bf16[8,2,2,896]{3,2,1,0:T(2,128)(2,1)}), bf16[8,2,2,896]{3,2,1,0:T(2,128)(2,1)S(1)}, u32[]{:S(2)}, u32[]{:S(2)}) async-start(bf16[8,2,2,896]{3,2,1,0:T(2,128)(2,1)} %broadcast_select_fusion), calls=%async_computation | async-start | bytes 114688 | tf_op jit(solution)/shard_map/all_to_all | solution.py:91
  27.1 9.2 %all-to-all-start.2 = ((bf16[8,2,2,896]{3,2,1,0:T(2,128)(2,1)}), bf16[8,2,2,896]{3,2,1,0:T(2,128)(2,1)S(1)}, u32[]{:S(2)}, u32[]{:S(2)}) async-start(bf16[8,2,2,896]{3,2,1,0:T(2,128)(2,1)} %select_convert_fusion), calls=%async_computation.2 | async-start | bytes 114688 | tf_op jit(solution)/shard_map/all_to_all | solution.py:98
  30.4 50.7 %all-reduce.3.cloned.1.call-start = ((), (), s32[]{:S(2)}) async-start(), calls=%async_computation.4 | async-start | bytes 393216 | tf_op jit(solution)/shard_map/psum | solution.py:122
  30.6 3.1 %copy-start.1 = (bf16[1,896,2048]{2,1,0:T(8,128)(2,1)S(1)}, bf16[1,896,2048]{2,1,0:T(8,128)(2,1)}, u32[]{:S(2)}) copy-start(bf16[1,896,2048]{2,1,0:T(8,128)(2,1)} %param.12) | copy-start | bytes 11010052
  84.8 2.0 %copy-start.2 = (bf16[1,896,2048]{2,1,0:T(8,128)(2,1)S(1)}, bf16[1,896,2048]{2,1,0:T(8,128)(2,1)}, u32[]{:S(2)}) copy-start(bf16[1,896,2048]{2,1,0:T(8,128)(2,1)} %param.12) | copy-start | bytes 11010052
  92.7 10.5 %all-to-all-start.1 = ((bf16[8,2,2,896]{3,2,1,0:T(2,128)(2,1)}), bf16[8,2,2,896]{3,2,1,0:T(2,128)(2,1)S(1)}, u32[]{:S(2)}, u32[]{:S(2)}) async-start(bf16[8,2,2,896]{3,2,1,0:T(2,128)(2,1)} %pad_maximum_fusion.3), calls=%async_computation.1 | async-start | bytes 114688 | tf_op jit(solution)/shard_map/all_to_all | solution.py:152
  103.2 9.2 %all-to-all-start.3 = ((bf16[8,2,2,896]{3,2,1,0:T(2,128)(2,1)}), bf16[8,2,2,896]{3,2,1,0:T(2,128)(2,1)S(1)}, u32[]{:S(2)}, u32[]{:S(2)}) async-start(bf16[8,2,2,896]{3,2,1,0:T(2,128)(2,1)} %pad_maximum_fusion.4), calls=%async_computation.3 | async-start | bytes 114688 | tf_op jit(solution)/shard_map/all_to_all | solution.py:153
Sparse Core Ops, SparseCore 0:
  39.0 42.0 all-reduce.2
where the time goes:
time: 122 us
  waiting for transfers between devices  52.1 us (43%)
  starting transfers between devices  17.9 us (15%)
  matrix products  16.8 us (14%)
  between operations  14.3 us (12%)
  local copies, waits for them, and re-layouts  11.1 us (9%)
  other arithmetic  9.6 us (8%)
    psum x1, waiting for transfers between devices, body(): lax.psum(grad_part.astype(jnp.bfloat16), 'dp').astype(jnp.float32)  42.2 us
    dot_general x4, matrix products, contract_first(): lax.dot_general(left, right, (((0,), (0,)), ((), ())), preferred_element_...  9.47 us
    all_to_all x1, starting transfers between devices, body(): lax.all_to_all(rows_in.reshape(expert_count, 2, CAP, share), 'expert', sp...  6.35 us
    all_to_all x1, waiting for transfers between devices, body(): lax.all_to_all(out_rows, 'expert', split_axis=0, concat_axis=0, tiled=True)  5.13 us
    all_to_all x1, starting transfers between devices, body(): lax.all_to_all(out_rows, 'expert', split_axis=0, concat_axis=0, tiled=True)  4.6 us
    all_to_all x1, starting transfers between devices, body(): lax.all_to_all(input_rows, 'expert', split_axis=0, concat_axis=0, tiled=T...  3.53 us
    all_to_all x1, starting transfers between devices, body(): lax.all_to_all(rows_grad.reshape(expert_count, 2, CAP, share), 'expert',...  3.35 us
    dot_general x4, matrix products, contract_last(): lax.dot_general(left, right, (((1,), (1,)), ((), ())), preferred_element_...  3.28 us
  transfers between devices with their start and end apart: 5, of which 5 were waited for; matrix products, arithmetic and copies ran while one was open for 11% of the time, Pallas kernels for 0%

commit v1 on v0

--- a/solution.py
+++ b/solution.py
@@ -4,6 +4,12 @@
 from jax.sharding import PartitionSpec as P
 
 CAP = 2
+
+
+def gather_and_add(x, mesh_axis):
+    parts = lax.all_gather(x, mesh_axis, axis=0, tiled=False)
+    result = parts.sum(axis=0)
+    return result
 
 
 def plan_block(flat_ids, hot, expert_count, capacity):
@@ -119,7 +125,7 @@
     )
     projected, hidden_grad = (
         lax.psum(proj_part.astype(jnp.bfloat16), "dp").astype(jnp.float32),
-        lax.psum(grad_part.astype(jnp.bfloat16), "dp").astype(jnp.float32),
+        gather_and_add(grad_part.astype(jnp.bfloat16), "dp").astype(jnp.float32),
     )
     gate_part, up_part, sigmoid_gate, hidden = activate(projected)
     pair_grad = pair_grads(hidden_grad, gate_part, up_part, sigmoid_gate)

time: 122 us -> 119 us (0.975)
  waiting for transfers between devices: 52.1 us -> 41.3 us
  blocking collectives: 0 us -> 9.04 us
  other arithmetic: 9.6 us -> 8.17 us
    psum x1, waiting for transfers between devices: 42.2 us -> 32.1 us  [body(): lax.psum(proj_part.astype(jnp.bfloat16), 'dp').astype(jnp.float32)]
    all_gather x0 -> x1, blocking collectives: none -> 9.04 us  [gather_and_add(): parts = lax.all_gather(x, mesh_axis, axis=0, tiled=False)]
  transfers between devices with their start and end apart: 5 -> 5, of which waited for: 5 -> 5; matrix products, arithmetic and copies ran while one was open for 11% -> 13% of each run, Pallas kernels for 0% -> 0%
where the time goes in v1:
time: 119 us
  waiting for transfers between devices  41.3 us (35%)
  starting transfers between devices  17.9 us (15%)
  matrix products  16.8 us (14%)
  between operations  14.3 us (12%)
  local copies, waits for them, and re-layouts  11.1 us (9%)
  blocking collectives  9.04 us (8%)
  other arithmetic  8.17 us (7%)
    psum x1, waiting for transfers between devices, body(): lax.psum(proj_part.astype(jnp.bfloat16), 'dp').astype(jnp.float32)  32.1 us
    dot_general x4, matrix products, contract_first(): lax.dot_general(left, right, (((0,), (0,)), ((), ())), preferred_element_...  9.46 us
    all_gather x1, blocking collectives, gather_and_add(): parts = lax.all_gather(x, mesh_axis, axis=0, tiled=False)  9.04 us
    all_to_all x1, starting transfers between devices, body(): lax.all_to_all(rows_in.reshape(expert_count, 2, CAP, share), 'expert', sp...  6.35 us
    all_to_all x1, waiting for transfers between devices, body(): lax.all_to_all(out_rows, 'expert', split_axis=0, concat_axis=0, tiled=True)  5.13 us
    all_to_all x1, starting transfers between devices, body(): lax.all_to_all(out_rows, 'expert', split_axis=0, concat_axis=0, tiled=True)  4.6 us
    all_to_all x1, starting transfers between devices, body(): lax.all_to_all(input_rows, 'expert', split_axis=0, concat_axis=0, tiled=T...  3.53 us
    all_to_all x1, starting transfers between devices, body(): lax.all_to_all(rows_grad.reshape(expert_count, 2, CAP, share), 'expert',...  3.35 us
  transfers between devices with their start and end apart: 5, of which 5 were waited for; matrix products, arithmetic and copies ran while one was open for 13% of the time, Pallas kernels for 0%

profile of v1, /device:TPU:0, one launch (start us, length us, event | category | flops | bytes accessed | tf_op | source)
XLA Modules:
  0.0 118.6 jit_solution(12167412400064172413)
XLA Ops:
  7.2 0.9 copy.24
  8.4 0.6 reduce-window.14
  9.0 0.2 slice_reduce_fusion.1
  9.2 0.8 select_reduce_fusion
  10.0 0.6 reduce-window.16
  10.6 0.2 slice_reduce_fusion
  10.8 0.1 fusion.63
  11.0 1.4 %scatter_custom_fusion = s32[33]{0:T(128)S(1)} fusion(s32[256]{0:T(256)S(1)} %bitcast.110, s32[256]{0:T(256)S(1)} %iota.19, s32[]{:T(128)} %constant.65.clone.1), kind=kCustom, calls=%fused_computation.137 | custom fusion | bytes 136 | tf_op jit(solution)/shard_map/scatter | solution.py:35
  12.4 1.5 %gather_fusion = bf16[32,896]{1,0:T(8,128)(2,1)S(1)} fusion(bf16[32,896]{1,0:T(8,128)(2,1)} %param.7, s32[1024]{0:T(1024)S(1)} %get-tuple-element.26), kind=kCustom, calls=%fused_computation | custom fusion | bytes 114816 | tf_op jit(solution)/shard_map/gather | solution.py:44
  14.0 0.1 lt.116
  14.1 0.8 broadcast_select_fusion
  14.8 6.4 %all-to-all-start = ((bf16[8,2,2,896]{3,2,1,0:T(2,128)(2,1)}), bf16[8,2,2,896]{3,2,1,0:T(2,128)(2,1)S(1)}, u32[]{:S(2)}, u32[]{:S(2)}) async-start(bf16[8,2,2,896]{3,2,1,0:T(2,128)(2,1)} %broadcast_select_fusion), calls=%async_computation | async-start | bytes 114688 | tf_op jit(solution)/shard_map/all_to_all | solution.py:97
  21.2 1.5 %gather_fusion.3 = bf16[32,896]{1,0:T(8,128)(2,1)S(1)} fusion(bf16[32,896]{1,0:T(8,128)(2,1)} %param.8, s32[1024]{0:T(1024)S(1)} %get-tuple-element.26), kind=kCustom, calls=%fused_computation.3 | custom fusion | bytes 114816 | tf_op jit(solution)/shard_map/gather | solution.py:45
  22.8 0.8 copy.31
  23.6 0.7 gather_fusion.2
  24.3 0.1 mul.92
  24.4 0.1 lt.110
  24.5 0.8 select_convert_fusion
  25.3 1.8 %all-to-all-done = bf16[8,2,2,896]{3,2,1,0:T(2,128)(2,1)S(1)} async-done(((bf16[8,2,2,896]{3,2,1,0:T(2,128)(2,1)}), bf16[8,2,2,896]{3,2,1,0:T(2,128)(2,1)S(1)}, u32[]{:S(2)}, u32[]{:S(2)}) %all-to-all-start) | async-done | bytes 57376 | tf_op jit(solution)/shard_map/all_to_all | solution.py:97
  27.1 3.4 %all-to-all-start.2 = ((bf16[8,2,2,896]{3,2,1,0:T(2,128)(2,1)}), bf16[8,2,2,896]{3,2,1,0:T(2,128)(2,1)S(1)}, u32[]{:S(2)}, u32[]{:S(2)}) async-start(bf16[8,2,2,896]{3,2,1,0:T(2,128)(2,1)} %select_convert_fusion), calls=%async_computation.2 | async-start | bytes 114688 | tf_op jit(solution)/shard_map/all_to_all | solution.py:104
  30.6 2.8 %fusion.12 = bf16[16,2048]{1,0:T(8,128)(2,1)S(1)} fusion(bf16[16,896]{1,0:T(8,128)(2,1)S(1)} %reshape_squeeze.13, bf16[1,896,2048]{2,1,0:T(8,128)(2,1)} %param.12), kind=kOutput, calls=%fused_computation.19 | convolution fusion | flops 58753024 | bytes 3764224 | tf_op jit(solution)/shard_map/dot_general | solution.py:119
  33.4 0.3 copy-done.1
  33.7 0.6 fusion.9
  34.3 0.7 pad_maximum_fusion
  35.0 1.3 %all-to-all-done.2 = bf16[8,2,2,896]{3,2,1,0:T(2,128)(2,1)S(1)} async-done(((bf16[8,2,2,896]{3,2,1,0:T(2,128)(2,1)}), bf16[8,2,2,896]{3,2,1,0:T(2,128)(2,1)S(1)}, u32[]{:S(2)}, u32[]{:S(2)}) %all-to-all-start.2) | async-done | bytes 57376 | tf_op jit(solution)/shard_map/all_to_all | solution.py:104
  36.4 0.6 fusion.42
  37.0 0.6 fusion.45
  37.6 9.0 %all_gather.4 = bf16[4,32,1024]{2,1,0:T(8,128)(2,1)S(1)} all-gather(bf16[1,32,1024]{2,1,0:T(8,128)(2,1)S(1)} %pad_maximum_fusion.2), channel_id=1, replica_groups=mesh['dp'=4,'expert'=8] {'dp'}, dimensions={0}, use_global_device_ids=true | all-gather | bytes 327680 | tf_op jit(solution)/shard_map/all_gather | solution.py:10
  46.7 32.1 %all-reduce.2.cloned.1.call-done = bf16[32,2048]{1,0:T(8,128)(2,1)} async-done(((bf16[32,2048]{1,0:T(8,128)(2,1)}), bf16[32,2048]{1,0:T(8,128)(2,1)}) %all-reduce.2.cloned.1.call-update) | async-done | bytes 131088 | tf_op jit(solution)/shard_map/psum | solution.py:127
  78.8 0.9 convert_element_type.102
  79.8 1.9 %convolution_convert_fusion.1 = bf16[1024,896]{1,0:T(8,128)(2,1)} fusion(bf16[16,896]{1,0:T(8,128)(2,1)S(1)} %reshape_squeeze.15, bf16[32,1024]{1,0:T(8,128)(2,1)S(1)} %get-tuple-element.18), kind=kOutput, calls=%fused_computation.28 | convolution fusion | flops 30277632 | bytes 1896448 | tf_op jit(solution)/shard_map/dot_general | solution.py:72
  81.7 0.3 fusion.30
  82.0 0.4 fusion.33
  82.4 1.2 convolution_convert_fusion
  83.6 0.2 copy-done.2
  83.7 1.0 fusion.36
  84.8 1.1 fusion.39
  85.8 3.0 %fusion.8 = bf16[1,896,2048]{2,1,0:T(8,128)(2,1)} fusion(bf16[896,2048]{1,0:T(8,128)(2,1)S(1)} %convolution_convert_fusion, bf16[16,896]{1,0:T(8,128)(2,1)S(1)} %reshape_squeeze.12, bf16[32,1024]{1,0:T(8,128)(2,1)S(1)} %get-tuple-element.16, bf16[32,1024]{1,0:T(8,128)(2,1)S(1)} %get-tuple-element.17), kind=kOutput, calls=%fused_computation.17 | convolution fusion | flops 64356352 | bytes 7499776 | tf_op jit(solution)/shard_map/dot_general | solution.py:72
  88.9 0.7 pad_maximum_fusion.3
  89.6 4.6 %all-to-all-start.1 = ((bf16[8,2,2,896]{3,2,1,0:T(2,128)(2,1)}), bf16[8,2,2,896]{3,2,1,0:T(2,128)(2,1)S(1)}, u32[]{:S(2)}, u32[]{:S(2)}) async-start(bf16[8,2,2,896]{3,2,1,0:T(2,128)(2,1)} %pad_maximum_fusion.3), calls=%async_computation.1 | async-start | bytes 114688 | tf_op jit(solution)/shard_map/all_to_all | solution.py:158
  94.2 0.7 pad_maximum_fusion.4
  94.9 5.1 %all-to-all-done.1 = bf16[8,2,2,896]{3,2,1,0:T(2,128)(2,1)S(1)} async-done(((bf16[8,2,2,896]{3,2,1,0:T(2,128)(2,1)}), bf16[8,2,2,896]{3,2,1,0:T(2,128)(2,1)S(1)}, u32[]{:S(2)}, u32[]{:S(2)}) %all-to-all-start.1) | async-done | bytes 57376 | tf_op jit(solution)/shard_map/all_to_all | solution.py:158
  100.1 3.5 %all-to-all-start.3 = ((bf16[8,2,2,896]{3,2,1,0:T(2,128)(2,1)}), bf16[8,2,2,896]{3,2,1,0:T(2,128)(2,1)S(1)}, u32[]{:S(2)}, u32[]{:S(2)}) async-start(bf16[8,2,2,896]{3,2,1,0:T(2,128)(2,1)} %pad_maximum_fusion.4), calls=%async_computation.3 | async-start | bytes 114688 | tf_op jit(solution)/shard_map/all_to_all | solution.py:159
  103.6 3.4 %fusion.23 = bf16[1,1024,896]{2,1,0:T(8,128)(2,1)} fusion(bf16[1024,896]{1,0:T(8,128)(2,1)} %convolution_convert_fusion.1, bf16[16,896]{1,0:T(8,128)(2,1)S(1)} %reshape_squeeze.14, bf16[32,1024]{1,0:T(8,128)(2,1)S(1)} %get-tuple-element.18), kind=kOutput, calls=%fused_computation.29 | convolution fusion | flops 32112640 | bytes 3731456 | tf_op jit(solution)/shard_map/dot_general | solution.py:72
  107.0 1.2 %gather_fusion.1 = bf16[256,896]{1,0:T(8,128)(2,1)S(1)} fusion(bf16[32,896]{1,0:T(8,128)(2,1)S(1)} %reshape.324, s32[1024]{0:T(1024)S(1)} %pad_clamp_fusion.1), kind=kCustom, calls=%fused_computation.1 | custom fusion | bytes 918528 | tf_op jit(solution)/shard_map/gather | solution.py:164
  108.2 1.0 all-to-all-done.3
  109.3 1.2 %gather_fusion.4 = bf16[256,896]{1,0:T(8,128)(2,1)S(1)} fusion(bf16[32,896]{1,0:T(8,128)(2,1)S(1)} %reshape.326, s32[1024]{0:T(1024)S(1)} %pad_clamp_fusion.1), kind=kCustom, calls=%fused_computation.4 | custom fusion | bytes 918528 | tf_op jit(solution)/shard_map/gather | solution.py:166
  110.5 1.3 %fusion.48 = (bf16[32,896]{1,0:T(8,128)(2,1)}, bf16[32,896]{1,0:T(8,128)(2,1)}) fusion(bf16[256,896]{1,0:T(8,128)(2,1)S(1)} %gather_fusion.4, pred[32,8]{1,0:T(8,128)(4,1)S(1)} %compare_and_fusion, f32[32,8]{1,0:T(8,128)S(1)} %copy.31, bf16[256,896]{1,0:T(8,128)(2,1)S(1)} %gather_fusion.1), kind=kLoop, calls=%fused_computation.39 | loop fusion | flops 1548288 | bytes 1033472 | tf_op jit(solution)/shard_map/reduce_sum | solution.py:170
  (46 shorter events, 1.2 us)
Async XLA Ops:
  7.2 29.2 %copy-start = (bf16[1,1024,896]{2,1,0:T(8,128)(2,1)S(1)}, bf16[1,1024,896]{2,1,0:T(8,128)(2,1)}, u32[]{:S(2)}) copy-start(bf16[1,1024,896]{2,1,0:T(8,128)(2,1)} %param.13) | copy-start | bytes 5505028
  14.8 12.2 %all-to-all-start = ((bf16[8,2,2,896]{3,2,1,0:T(2,128)(2,1)}), bf16[8,2,2,896]{3,2,1,0:T(2,128)(2,1)S(1)}, u32[]{:S(2)}, u32[]{:S(2)}) async-start(bf16[8,2,2,896]{3,2,1,0:T(2,128)(2,1)} %broadcast_select_fusion), calls=%async_computation | async-start | bytes 114688 | tf_op jit(solution)/shard_map/all_to_all | solution.py:97
  27.1 9.2 %all-to-all-start.2 = ((bf16[8,2,2,896]{3,2,1,0:T(2,128)(2,1)}), bf16[8,2,2,896]{3,2,1,0:T(2,128)(2,1)S(1)}, u32[]{:S(2)}, u32[]{:S(2)}) async-start(bf16[8,2,2,896]{3,2,1,0:T(2,128)(2,1)} %select_convert_fusion), calls=%async_computation.2 | async-start | bytes 114688 | tf_op jit(solution)/shard_map/all_to_all | solution.py:104
  30.4 48.4 %all-reduce.2.cloned.1.call-start = ((), (), s32[]{:S(2)}) async-start(), calls=%async_computation.4 | async-start | bytes 262144 | tf_op jit(solution)/shard_map/psum | solution.py:127
  30.6 3.1 %copy-start.1 = (bf16[1,896,2048]{2,1,0:T(8,128)(2,1)S(1)}, bf16[1,896,2048]{2,1,0:T(8,128)(2,1)}, u32[]{:S(2)}) copy-start(bf16[1,896,2048]{2,1,0:T(8,128)(2,1)} %param.12) | copy-start | bytes 11010052
  81.7 2.0 %copy-start.2 = (bf16[1,896,2048]{2,1,0:T(8,128)(2,1)S(1)}, bf16[1,896,2048]{2,1,0:T(8,128)(2,1)}, u32[]{:S(2)}) copy-start(bf16[1,896,2048]{2,1,0:T(8,128)(2,1)} %param.12) | copy-start | bytes 11010052
  89.6 10.5 %all-to-all-start.1 = ((bf16[8,2,2,896]{3,2,1,0:T(2,128)(2,1)}), bf16[8,2,2,896]{3,2,1,0:T(2,128)(2,1)S(1)}, u32[]{:S(2)}, u32[]{:S(2)}) async-start(bf16[8,2,2,896]{3,2,1,0:T(2,128)(2,1)} %pad_maximum_fusion.3), calls=%async_computation.1 | async-start | bytes 114688 | tf_op jit(solution)/shard_map/all_to_all | solution.py:158
  100.1 9.2 %all-to-all-start.3 = ((bf16[8,2,2,896]{3,2,1,0:T(2,128)(2,1)}), bf16[8,2,2,896]{3,2,1,0:T(2,128)(2,1)S(1)}, u32[]{:S(2)}, u32[]{:S(2)}) async-start(bf16[8,2,2,896]{3,2,1,0:T(2,128)(2,1)} %pad_maximum_fusion.4), calls=%async_computation.3 | async-start | bytes 114688 | tf_op jit(solution)/shard_map/all_to_all | solution.py:159
Sparse Core Ops, SparseCore 0:
  35.1 43.6 all-reduce.1
